TPU v7x, 512 devices: a whole 4x8x8 slice. The times are simulated.
512 devices in a mesh: section: 16 (over z, x_hi), dp: 32 (over y, x_lo, core).
Axes of the slice: x: 4 (x_hi: 2, x_lo: 2; x = x_hi * 2 + x_lo), y: 8, z: 8, core: 2. Of those that a mesh axis runs over, the one named last changes fastest.
Arguments:
- pending_predecessor_pair: float32 [16, 2, 32, 16, 16, 512], P('section', None, 'dp'), may hold values from -6 to 6
- incoming_stem_images: float32 [3, 32, 16, 16, 512], P(None, 'dp'), may hold values from -6 to 6
- spatial_filter_entries: float32 [16, 4, 9, 512], P('section', None, None, 'dp'), may hold values from -2 to 2
- mixing_matrix_entries: float32 [16, 4, 512, 512], P('section', None, 'dp'), may hold values from -0.25 to 0.25
Outputs:
- emitted: float32 [16, 4, 32, 16, 16, 512], P('section', None, 'dp')
All inputs are finite; a program needn't handle non-finite values.
Results may differ from a plain program's by a relative error of at most 0.00015.
Values sent between devices are 32-bit elements; how exact they have to be, the bound alone decides.
A program may use at most 64 MiB of HBM per device.

v0:
```python
import functools

import jax
import jax.numpy as jnp
from jax import lax
from jax.experimental import pallas as pl
from jax.experimental.pallas import tpu as pltpu
from jax.sharding import PartitionSpec as P

MESH = pl.DeviceIdType.MESH
F32, BF16 = jnp.float32, jnp.bfloat16
GRID = 16
PIX = GRID * GRID
TICKS = 4
ROWS = 16
OWN, PAIR, LATE = 0, 1, 2


def kernel(S, Y, C, pend, stem, blk, out, G, W3, A3, B3, taps, NEW, EAR, OUT, first, second,
           lsem, ssem, fsem, bsem, xssem, xsem, cssem, csem, nssem, nrsem, essem, ersem, osem):
    D = Y * 4
    T = C // 128
    EARLY, ALL = 4 * T + 1, 8 * T + 1
    KC = C // 2
    half = Y // 2
    sec, dp = lax.axis_index("section"), lax.axis_index("dp")
    y, xl, core = dp // 4, lax.rem(dp // 2, 2), lax.rem(dp, 2)
    yup, ydn = lax.rem(dp + 4, D), lax.rem(dp + D - 4, D)
    xpair, cpair = dp + 2 - 4 * xl, dp + 1 - 2 * core
    here = lambda d: {"section": sec, "dp": d}
    at = lambda s: {"section": s, "dp": dp}
    nxt, nxt2 = lax.rem(sec + 1, S), lax.rem(sec + 2, S)
    prv, prv2 = lax.rem(sec + S - 1, S), lax.rem(sec + S - 2, S)

    local = [
        pltpu.make_async_copy(blk, G.at[core, y, xl], lsem.at[0]),
        pltpu.make_async_copy(pend.at[0], EAR.at[0], lsem.at[1]),
        pltpu.make_async_copy(pend.at[1], NEW.at[0], lsem.at[2]),
    ]
    for c in local:
        c.start()
    stems_new = [pltpu.make_async_copy(stem.at[t - 1], NEW.at[t], lsem.at[2 + t]) for t in (1, 2, 3)]
    stems_ear = [pltpu.make_async_copy(stem.at[t - 1], EAR.at[t], lsem.at[5 + t]) for t in (1, 2, 3)]
    stems_one = [pltpu.make_async_copy(stem.at[t - 2], EAR.at[t], lsem.at[5 + t]) for t in (2, 3)]

    @pl.when(sec == 0)
    def _():
        for c in stems_new + stems_ear:
            c.start()

    @pl.when(sec == 1)
    def _():
        for c in stems_one:
            c.start()

    barrier = pltpu.get_barrier_semaphore()
    for d in (here(yup), here(ydn), here(xpair), here(cpair), at(nxt), at(prv), at(nxt2), at(prv2)):
        pl.semaphore_signal(barrier, inc=1, device_id=d, device_id_type=MESH)
    pl.semaphore_wait(barrier, 8)
    local[0].wait()

    sent = []

    def remote(src, dst, s, r, dev):
        return pltpu.make_async_remote_copy(src_ref=src, dst_ref=dst, send_sem=s, recv_sem=r,
                                            device_id=dev, device_id_type=MESH)

    def send(c):
        c.start()
        sent.append(c)

    def piece(cc, yy, xx, late):
        lo, n = (EARLY, ALL - EARLY) if late else (0, EARLY)
        return G.at[cc, yy, xx, pl.ds(lo, n)]

    def ring(way, stream, k):
        yy = lax.rem(y + Y - (k - 1), Y) if way == 0 else lax.rem(y + (k - 1), Y)
        xx = 1 - xl if stream == PAIR else xl
        p = piece(core, yy, xx, stream == LATE)
        sems = fsem if way == 0 else bsem
        return remote(p, p, ssem.at[way, stream, k - 1], sems.at[stream, k - 1], here(yup if way == 0 else ydn))

    def carried(way, stream, k):
        if k < half:
            return True
        return k == half and (way == 1 if stream == PAIR else way == 0)

    def arrived(way, stream, k):
        yy = lax.rem(y + Y - k, Y) if way == 0 else lax.rem(y + k, Y)
        xx = 1 - xl if stream == PAIR else xl
        p = piece(core, yy, xx, stream == LATE)
        sems = fsem if way == 0 else bsem
        remote(p, p, ssem.at[way, stream, k - 1], sems.at[stream, k - 1], here(ydn)).wait_recv()
        return yy, xx

    def slot(way, k):
        return 0 if k == 0 else (k if way == 0 else Y - k)

    def cross(way, k):
        yy = lax.rem(y + Y - k, Y) if way == 0 else lax.rem(y + k, Y)
        p = piece(core, yy, xl, True)
        n = slot(way, k)
        return remote(p, p, xssem.at[n], xsem.at[n], here(xpair))

    def crossed(way, k):
        yy = lax.rem(y + Y - k, Y) if way == 0 else lax.rem(y + k, Y)
        p = piece(core, yy, 1 - xl, True)
        n = slot(way, k)
        remote(p, p, xssem.at[n], xsem.at[n], here(xpair)).wait_recv()
        return yy, 1 - xl

    def share(yy, xx, late, way, k, pair):
        n = (2 if pair else 0) + (1 if late else 0)
        p = piece(core, yy, xx, late)
        send(remote(p, p, cssem.at[n, slot(way, k)], csem.at[n, slot(way, k)], here(cpair)))

    def shared(yy, xx, late, way, k, pair):
        n = (2 if pair else 0) + (1 if late else 0)
        p = piece(1 - core, yy, xx, late)
        remote(p, p, cssem.at[n, slot(way, k)], csem.at[n, slot(way, k)], here(cpair)).wait_recv()

    def split(cc, yy, xx, late):
        row = pl.multiple_of(((yy * 2 + xx) * 2 + cc) * ROWS, ROWS)
        base = EARLY if late else 0

        def step(m, carry):
            b = (2 if late else 0) + m
            for j in range(T):
                w = jnp.concatenate([G[cc, yy, xx, base + m * 2 * T + j], G[cc, yy, xx, base + m * 2 * T + T + j]], 0)
                hi = w.astype(BF16)
                lo = (w - hi.astype(F32)).astype(BF16)
                lanes = slice(128 * j, 128 * j + 128)
                W3[b, pl.ds(row, ROWS), lanes] = hi
                W3[b, pl.ds(pl.multiple_of(C + row, ROWS), ROWS), lanes] = hi
                W3[b, pl.ds(pl.multiple_of(2 * C + row, ROWS), ROWS), lanes] = lo
            return carry

        lax.fori_loop(0, 2, step, 0)

    own = piece(core, y, xl, False)
    send(remote(own, own, xssem.at[Y], xsem.at[Y], here(xpair)))
    for stream in (OWN, LATE):
        for way in (0, 1):
            if carried(way, stream, 1):
                send(ring(way, stream, 1))
    send(cross(0, 0))
    share(y, xl, False, 0, 0, False)
    share(y, xl, True, 0, 0, False)

    old_copy = remote(pend.at[1], EAR.at[1], essem.at[1], ersem.at[1], at(nxt))

    split(core, y, xl, False)
    split(core, y, xl, True)
    other = piece(core, y, 1 - xl, False)
    remote(other, other, xssem.at[Y], xsem.at[Y], here(xpair)).wait_recv()
    for way in (0, 1):
        if carried(way, PAIR, 1):
            send(ring(way, PAIR, 1))
    share(y, 1 - xl, False, 0, 0, True)
    split(core, y, 1 - xl, False)

    def tail(ways, k):
        for way in ways:
            yy, xx = crossed(way, k)
            share(yy, xx, True, way, k, True)
            split(core, yy, xx, True)
        for way in ways:
            yy = lax.rem(y + Y - k, Y) if way == 0 else lax.rem(y + k, Y)
            for pair in (False, True):
                xx = 1 - xl if pair else xl
                for late in (False, True):
                    shared(yy, xx, late, way, k, pair)
                    split(1 - core, yy, xx, late)

    for k in range(1, half + 1):
        got = []
        for stream in (LATE, OWN, PAIR):
            for way in (0, 1):
                if not carried(way, stream, k):
                    continue
                yy, xx = arrived(way, stream, k)
                if carried(way, stream, k + 1):
                    send(ring(way, stream, k + 1))
                late = stream == LATE
                w = 0 if k == half else way
                if late:
                    send(cross(w, k))
                share(yy, xx, late, w, k, stream == PAIR)
                got.append((yy, xx, late))
        if k == half:
            @pl.when(sec < S - 1)
            def _():
                old_copy.start()
        for yy, xx, late in got:
            split(core, yy, xx, late)
        tail((0,) if k == 1 else (0, 1), k - 1)
    tail((0,), half)

    lane = lax.broadcasted_iota(jnp.int32, (8, 128), 1) // ROWS

    def gather_taps(g, carry):
        lanes = pl.ds(pl.multiple_of(g * 128, 128), 128)
        tiles = [G[e % 2, 2 * g + e // 4, (e // 2) % 2, EARLY - 1] for e in range(8)]
        for q in range(8):
            row = jnp.zeros((8, 128), F32)
            for e in range(8):
                shift = ((e - q) % 8) * ROWS
                moved = pltpu.roll(tiles[e], shift, 1) if shift else tiles[e]
                row = jnp.where(lane == e, moved, row)
            taps[q, :, lanes] = row
        return carry

    lax.fori_loop(0, T, gather_taps, 0)

    for c in local[1:]:
        c.wait()

    @pl.when(sec == 0)
    def _():
        for c in stems_new + stems_ear:
            c.wait()

    @pl.when(sec == 1)
    def _():
        for c in stems_one:
            c.wait()

    def tap(b, t, kc):
        n = 9 * b + t
        return taps[n % 8, n // 8:n // 8 + 1, kc * KC:(kc + 1) * KC].reshape(1, 1, KC)

    col = lax.broadcasted_iota(jnp.int32, (1, GRID, KC), 1)

    def depthwise(v, b, kc, acts):
        v = jnp.maximum(v.reshape(GRID, GRID, KC), 0.0)
        left, right = pltpu.roll(v, 1, 1), pltpu.roll(v, GRID - 1, 1)
        rows = []
        for i in range(3):
            kl = jnp.where(col == 0, 0.0, jnp.broadcast_to(tap(b, 3 * i, kc), (1, GRID, KC)))
            kr = jnp.where(col == GRID - 1, 0.0, jnp.broadcast_to(tap(b, 3 * i + 2, kc), (1, GRID, KC)))
            rows.append(left * kl + v * tap(b, 3 * i + 1, kc) + right * kr)
        zero = jnp.zeros((1, GRID, KC), F32)
        total = (jnp.concatenate([zero, rows[0][:GRID - 1]], 0) + rows[1]
                 + jnp.concatenate([rows[2][1:], zero], 0)).reshape(PIX, KC)
        hi = total.astype(BF16)
        lo = (total - hi.astype(F32)).astype(BF16)
        acts[:, kc * KC:(kc + 1) * KC] = hi
        acts[:, C + kc * KC:C + (kc + 1) * KC] = lo
        acts[:, 2 * C + kc * KC:2 * C + (kc + 1) * KC] = hi

    def product(acts, b, nc):
        return jnp.dot(acts[...], W3[b, :, nc * KC:(nc + 1) * KC], preferred_element_type=F32)

    part = lambda nc: slice(nc * KC, (nc + 1) * KC)
    span = lambda nc: pl.ds(nc * KC, KC)

    def new_copy(t, nc):
        return remote(OUT.at[t, :, span(nc)], NEW.at[t + 1, :, span(nc)], nssem.at[t, nc], nrsem.at[t + 1, nc], at(nxt))

    def ear_copy(t):
        return remote(OUT.at[t], EAR.at[t + 2], essem.at[t + 2], ersem.at[t + 2], at(nxt2))

    def out_copy(t):
        return pltpu.make_async_copy(OUT.at[t], out.at[t], osem.at[t])

    def tick(t, carry):
        @pl.when(((t == 1) & (sec > 0)) | ((t > 1) & (sec > 1)))
        def _():
            remote(EAR.at[t], EAR.at[t], essem.at[t], ersem.at[t], at(prv)).wait_recv()

        for kc in (0, 1):
            depthwise(EAR[t, :, part(kc)], 1, kc, B3)
        for nc in (0, 1):
            first[:, part(nc)] = product(B3, 1, nc)
        for kc in (0, 1):
            @pl.when((t > 0) & (sec > 0))
            def _():
                remote(NEW.at[t, :, span(kc)], NEW.at[t, :, span(kc)], nssem.at[t, kc], nrsem.at[t, kc], at(prv)).wait_recv()

            depthwise(NEW[t, :, part(kc)], 0, kc, A3)
        for nc in (0, 1):
            first[:, part(nc)] += product(A3, 0, nc)
        for kc in (0, 1):
            depthwise(first[:, part(kc)], 2, kc, B3)
        for nc in (0, 1):
            second[:, part(nc)] = product(B3, 2, nc) + NEW[t, :, part(nc)]
        for kc in (0, 1):
            depthwise(second[:, part(kc)], 3, kc, A3)
        for nc in (0, 1):
            OUT[t, :, part(nc)] = product(A3, 3, nc) + first[:, part(nc)]

            @pl.when((t < TICKS - 1) & (sec < S - 1))
            def _():
                new_copy(t, nc).start()

        @pl.when((t < TICKS - 2) & (sec < S - 2))
        def _():
            ear_copy(t).start()

        out_copy(t).start()
        return carry

    lax.fori_loop(0, TICKS, tick, 0)

    for c in sent:
        c.wait_send()

    @pl.when(sec < S - 1)
    def _():
        old_copy.wait_send()
        for t in range(TICKS - 1):
            for nc in (0, 1):
                new_copy(t, nc).wait_send()

    @pl.when(sec < S - 2)
    def _():
        for t in range(TICKS - 2):
            ear_copy(t).wait_send()

    for t in range(TICKS):
        out_copy(t).wait()


def body(S, Y, pend, stem, spatial, mixing):
    C = mixing.shape[-1]
    T = C // 128
    pend = pend.reshape(2, PIX, C)
    stem = stem.reshape(TICKS - 1, PIX, C)
    flat = jnp.pad(spatial.reshape(36, ROWS), ((0, 28), (0, 0))).reshape(1, 8, 128)
    tiles = mixing.reshape(4, 2, 8, T, 128).transpose(0, 1, 3, 2, 4).reshape(8 * T, 8, 128)
    blk = jnp.concatenate([tiles[:4 * T], flat, tiles[4 * T:]], 0)
    dma = pltpu.SemaphoreType.DMA
    any_ = pl.BlockSpec(memory_space=pl.ANY)
    half = Y // 2
    out = pl.pallas_call(
        functools.partial(kernel, S, Y, C),
        out_shape=jax.ShapeDtypeStruct((TICKS, PIX, C), F32),
        in_specs=[any_] * 3,
        out_specs=any_,
        scratch_shapes=[
            pltpu.VMEM((2, Y, 2, 8 * T + 1, 8, 128), F32),
            pltpu.VMEM((4, 3 * C, C), BF16),
            pltpu.VMEM((PIX, 3 * C), BF16),
            pltpu.VMEM((PIX, 3 * C), BF16),
            pltpu.VMEM((8, 8, C), F32),
            pltpu.VMEM((TICKS, PIX, C), F32),
            pltpu.VMEM((TICKS, PIX, C), F32),
            pltpu.VMEM((TICKS, PIX, C), F32),
            pltpu.VMEM((PIX, C), F32),
            pltpu.VMEM((PIX, C), F32),
            dma((9,)),
            dma((2, 3, half)),
            dma((3, half)),
            dma((3, half)),
            dma((Y + 1,)),
            dma((Y + 1,)),
            dma((4, Y)),
            dma((4, Y)),
            dma((TICKS, 2)),
            dma((TICKS, 2)),
            dma((TICKS,)),
            dma((TICKS,)),
            dma((TICKS,)),
        ],
        compiler_params=pltpu.CompilerParams(collective_id=0, has_side_effects=True, vmem_limit_bytes=60 << 20),
        name="relay",
    )(pend, stem, blk)
    return out.reshape(1, TICKS, 1, GRID, GRID, C)


def solution(mesh):
    S, D = mesh.shape["section"], mesh.shape["dp"]
    placed = (
        P("section", None, "dp", None, None, None),
        P(None, "dp", None, None, None),
        P("section", None, None, "dp"),
        P("section", None, "dp", None),
    )
    return jax.shard_map(
        functools.partial(body, S, D // 4),
        mesh=mesh,
        in_specs=placed,
        out_specs=P("section", None, "dp", None, None, None),
        check_vma=False,
    )
```

profile of v0, /device:TPU:195, one launch (start us, length us, event | category | flops | bytes accessed | tf_op | source)
XLA Modules:
  0.0 123.6 jit_solution(4705310387018585868)
XLA Ops:
  0.0 0.7 copy.10
  0.7 0.1 reshape.25
  0.8 0.9 fusion
  1.7 0.7 pad_maximum_fusion.blk
  2.4 118.0 %relay.1 = f32[4,256,512]{2,1,0:T(8,128)} custom-call(f32[2,256,512]{2,1,0:T(8,128)} %bitcast.12, f32[3,256,512]{2,1,0:T(8,128)} %bitcast.11, f32[33,8,128]{2,1,0:T(8,128)} %pad_maximum_fusion.blk), custom_call_target="tpu_custom_call" | custom-call | tf_op jit(solution)/shard_map/relay/pallas_call | solution.py:335
  120.4 3.2 %copy.13 = f32[1,4,1,16,16,512]{5,4,3,2,1,0:T(8,128)} copy(f32[1,4,1,16,16,512]{5,4,3,2,1,0:T(8,128)} %bitcast.10) | data formatting | bytes 4194304
  (2 shorter events, 0.0 us)
where the time goes:
time: 124 us
  Pallas kernels  118 us (95%)
  local copies, waits for them, and re-layouts  4.92 us (4%)
    pallas_call x1, Pallas kernels, body(): pl.pallas_call(functools.partial(kernel, S, Y, C), out_shape=jax.ShapeDty...  118 us
    unnamed x3, local copies, waits for them, and re-layouts  3.95 us

commit v1 on v0

--- a/solution.py
+++ b/solution.py
@@ -16,8 +16,8 @@
 OWN, PAIR, LATE = 0, 1, 2
 
 
-def kernel(S, Y, C, pend, stem, blk, out, G, W3, A3, B3, taps, NEW, EAR, OUT, first, second,
-           lsem, ssem, fsem, bsem, xssem, xsem, cssem, csem, nssem, nrsem, essem, ersem, osem):
+def kernel(S, Y, C, pend, stem, blk, OUT, G, W3, A3, B3, taps, NEW, EAR, first, second,
+           lsem, ssem, fsem, bsem, xssem, xsem, cssem, csem, nssem, nrsem, essem, ersem):
     D = Y * 4
     T = C // 128
     EARLY, ALL = 4 * T + 1, 8 * T + 1
@@ -148,6 +148,10 @@
     share(y, xl, True, 0, 0, False)
 
     old_copy = remote(pend.at[1], EAR.at[1], essem.at[1], ersem.at[1], at(nxt))
+
+    @pl.when(sec < S - 1)
+    def _():
+        old_copy.start()
 
     split(core, y, xl, False)
     split(core, y, xl, True)
@@ -187,10 +191,6 @@
                     send(cross(w, k))
                 share(yy, xx, late, w, k, stream == PAIR)
                 got.append((yy, xx, late))
-        if k == half:
-            @pl.when(sec < S - 1)
-            def _():
-                old_copy.start()
         for yy, xx, late in got:
             split(core, yy, xx, late)
         tail((0,) if k == 1 else (0, 1), k - 1)
@@ -260,9 +260,6 @@
     def ear_copy(t):
         return remote(OUT.at[t], EAR.at[t + 2], essem.at[t + 2], ersem.at[t + 2], at(nxt2))
 
-    def out_copy(t):
-        return pltpu.make_async_copy(OUT.at[t], out.at[t], osem.at[t])
-
     def tick(t, carry):
         @pl.when(((t == 1) & (sec > 0)) | ((t > 1) & (sec > 1)))
         def _():
@@ -297,7 +294,6 @@
         def _():
             ear_copy(t).start()
 
-        out_copy(t).start()
         return carry
 
     lax.fori_loop(0, TICKS, tick, 0)
@@ -316,9 +312,6 @@
     def _():
         for t in range(TICKS - 2):
             ear_copy(t).wait_send()
-
-    for t in range(TICKS):
-        out_copy(t).wait()
 
 
 def body(S, Y, pend, stem, spatial, mixing):
@@ -336,14 +329,13 @@
         functools.partial(kernel, S, Y, C),
         out_shape=jax.ShapeDtypeStruct((TICKS, PIX, C), F32),
         in_specs=[any_] * 3,
-        out_specs=any_,
+        out_specs=pl.BlockSpec(memory_space=pltpu.VMEM),
         scratch_shapes=[
             pltpu.VMEM((2, Y, 2, 8 * T + 1, 8, 128), F32),
             pltpu.VMEM((4, 3 * C, C), BF16),
             pltpu.VMEM((PIX, 3 * C), BF16),
             pltpu.VMEM((PIX, 3 * C), BF16),
             pltpu.VMEM((8, 8, C), F32),
-            pltpu.VMEM((TICKS, PIX, C), F32),
             pltpu.VMEM((TICKS, PIX, C), F32),
             pltpu.VMEM((TICKS, PIX, C), F32),
             pltpu.VMEM((PIX, C), F32),
@@ -360,9 +352,8 @@
             dma((TICKS, 2)),
             dma((TICKS,)),
             dma((TICKS,)),
-            dma((TICKS,)),
         ],
-        compiler_params=pltpu.CompilerParams(collective_id=0, has_side_effects=True, vmem_limit_bytes=60 << 20),
+        compiler_params=pltpu.CompilerParams(collective_id=0, has_side_effects=True, vmem_limit_bytes=24 << 20),
         name="relay",
     )(pend, stem, blk)
     return out.reshape(1, TICKS, 1, GRID, GRID, C)

time: 124 us -> 112 us (0.903)
  the two profiles are of different devices: /device:TPU:195 before, /device:TPU:384 now
where the time goes in v1:
time: 112 us
  Pallas kernels  107 us (96%)
  local copies, waits for them, and re-layouts  5.65 us (5%)
    pallas_call x1, Pallas kernels, body(): pl.pallas_call(functools.partial(kernel, S, Y, C), out_shape=jax.ShapeDty...  107 us
    unnamed x7, local copies, waits for them, and re-layouts  4.68 us

profile of v1, /device:TPU:384, one launch (start us, length us, event | category | flops | bytes accessed | tf_op | source)
XLA Modules:
  0.0 112.2 jit_solution(1953268565885329918)
XLA Ops:
  0.0 0.7 copy.10
  0.7 0.1 reshape.25
  0.8 0.9 fusion
  1.7 0.0 copy-start
  1.7 1.4 %copy-done = f32[3,1,16,16,512]{4,3,2,1,0:T(8,128)S(1)} copy-done((f32[3,1,16,16,512]{4,3,2,1,0:T(8,128)S(1)}, f32[3,1,16,16,512]{4,3,2,1,0:T(8,128)}, u32[]{:S(2)}) %copy-start) | copy-done | bytes 1572888
  3.1 0.0 copy-start.1
  3.1 1.2 %copy-done.1 = f32[1,2,1,16,16,512]{5,4,3,2,1,0:T(8,128)S(1)} copy-done((f32[1,2,1,16,16,512]{5,4,3,2,1,0:T(8,128)S(1)}, f32[1,2,1,16,16,512]{5,4,3,2,1,0:T(8,128)}, u32[]{:S(2)}) %copy-start.1) | copy-done | bytes 1048600
  4.4 106.5 %relay.1 = f32[4,256,512]{2,1,0:T(8,128)S(1)} custom-call(f32[2,256,512]{2,1,0:T(8,128)S(1)} %bitcast.12, f32[3,256,512]{2,1,0:T(8,128)S(1)} %bitcast.11, f32[33,8,128]{2,1,0:T(8,128)S(1)} %pad_maximum_fusion.blk), custom_call_target="tpu_custom_call" | custom-call | tf_op jit(solution)/shard_map/relay/pallas_call | solution.py:328
  110.9 1.3 %copy.13 = f32[1,4,1,16,16,512]{5,4,3,2,1,0:T(8,128)} copy(f32[1,4,1,16,16,512]{5,4,3,2,1,0:T(8,128)S(1)} %bitcast.10) | data formatting | bytes 4194304
  (3 shorter events, 0.0 us)
Async XLA Ops:
  1.7 1.4 %copy-start = (f32[3,1,16,16,512]{4,3,2,1,0:T(8,128)S(1)}, f32[3,1,16,16,512]{4,3,2,1,0:T(8,128)}, u32[]{:S(2)}) copy-start(f32[3,1,16,16,512]{4,3,2,1,0:T(8,128)} %param.5) | copy-start | bytes 4718596
  3.1 1.2 %copy-start.1 = (f32[1,2,1,16,16,512]{5,4,3,2,1,0:T(8,128)S(1)}, f32[1,2,1,16,16,512]{5,4,3,2,1,0:T(8,128)}, u32[]{:S(2)}) copy-start(f32[1,2,1,16,16,512]{5,4,3,2,1,0:T(8,128)} %param.4) | copy-start | bytes 3145732

commit v2 on v1

v2 whole, which is shorter than its diff:
```python
import functools

import jax
import jax.numpy as jnp
from jax import lax
from jax.experimental import pallas as pl
from jax.experimental.pallas import tpu as pltpu
from jax.sharding import PartitionSpec as P

MESH = pl.DeviceIdType.MESH
F32, BF16 = jnp.float32, jnp.bfloat16
GRID = 16
PIX = GRID * GRID
TICKS = 4
ROWS = 16
OWN, PAIR, LATE, TWIN, TWIN_PAIR = range(5)


def kernel(S, Y, C, pend, stem, blk, OUT, G, W3, A3, B3, taps, BUF, first, second,
           lsem, ssem, rsem, xssem, xsem, ossem, orsem, cssem, csem, mssem, mrsem):
    D = Y * 4
    T = C // 128
    EARLY, ALL = 4 * T + 1, 8 * T + 1
    KC = C // 2
    half = Y // 2
    sec, dp = lax.axis_index("section"), lax.axis_index("dp")
    odd = lax.rem(sec, 2)
    y, xl, core = dp // 4, lax.rem(dp // 2, 2), lax.rem(dp, 2)
    yup, ydn = lax.rem(dp + 4, D), lax.rem(dp + D - 4, D)
    xpair, cpair = dp + 2 - 4 * xl, dp + 1 - 2 * core
    twin = sec + 1 - 2 * odd
    here = lambda d: {"section": sec, "dp": d}
    at = lambda s: {"section": s, "dp": dp}
    there = lambda d: {"section": twin, "dp": d}
    nxt, nxt2 = lax.rem(sec + 1, S), lax.rem(sec + 2, S)
    prv, prv2 = lax.rem(sec + S - 1, S), lax.rem(sec + S - 2, S)

    local = [
        pltpu.make_async_copy(blk, G.at[0, core, y, xl], lsem.at[0]),
        pltpu.make_async_copy(pend.at[0], BUF.at[0], lsem.at[1]),
        pltpu.make_async_copy(pend.at[1], BUF.at[1], lsem.at[2]),
    ]
    for c in local:
        c.start()
    stems_zero = [pltpu.make_async_copy(stem.at[n], BUF.at[m], lsem.at[m]) for n, m in ((1, 4), (1, 5), (2, 6), (2, 7))]
    stems_one = [pltpu.make_async_copy(stem.at[n], BUF.at[m], lsem.at[m + 6]) for n, m in ((0, 2), (0, 3), (1, 6))]

    @pl.when(sec == 0)
    def _():
        for c in stems_zero:
            c.start()

    @pl.when(sec == 1)
    def _():
        for c in stems_one:
            c.start()

    barrier = pltpu.get_barrier_semaphore()
    partners = (here(yup), here(ydn), here(xpair), here(cpair), there(dp), there(xpair), at(nxt), at(prv), at(nxt2), at(prv2))
    for d in partners:
        pl.semaphore_signal(barrier, inc=1, device_id=d, device_id_type=MESH)
    pl.semaphore_wait(barrier, len(partners))
    local[0].wait()

    sent = []

    def remote(src, dst, s, r, dev):
        return pltpu.make_async_remote_copy(src_ref=src, dst_ref=dst, send_sem=s, recv_sem=r,
                                            device_id=dev, device_id_type=MESH)

    def send(c):
        c.start()
        sent.append(c)

    def piece(p, cc, yy, xx, late):
        lo, n = (EARLY, ALL - EARLY) if late else (0, EARLY)
        return G.at[p, cc, yy, xx, pl.ds(lo, n)]

    def column(stream):
        return xl if stream in (OWN, LATE, TWIN) else 1 - xl

    def place(way, k):
        return lax.rem(y + Y - k, Y) if way == 0 else lax.rem(y + k, Y)

    def ring_piece(stream, yy):
        return piece(1 if stream >= TWIN else 0, core, yy, column(stream), stream == LATE)

    def ring(way, stream, k):
        p = ring_piece(stream, place(way, k - 1))
        return remote(p, p, ssem.at[way, stream, k - 1], rsem.at[way, stream, k - 1], here(yup if way == 0 else ydn))

    def carried(way, stream, k):
        return k < half or (k == half and way == (1 if stream in (PAIR, TWIN_PAIR) else 0))

    def arrived(way, stream, k):
        yy = place(way, k)
        p = ring_piece(stream, yy)
        remote(p, p, ssem.at[way, stream, k - 1], rsem.at[way, stream, k - 1], here(ydn)).wait_recv()
        return yy

    def slot(way, k):
        return 0 if k == 0 else (k if way == 0 else Y - k)

    def cross(way, k):
        p = piece(0, core, place(way, k), xl, True)
        return remote(p, p, xssem.at[slot(way, k)], xsem.at[slot(way, k)], here(xpair))

    def crossed(way, k):
        p = piece(0, core, place(way, k), 1 - xl, True)
        remote(p, p, xssem.at[slot(way, k)], xsem.at[slot(way, k)], here(xpair)).wait_recv()

    def over(far, yy, late, n):
        return remote(piece(0, core, yy, xl, late), piece(1, core, yy, xl, late), ossem.at[far, n], orsem.at[far, n],
                      there(xpair if far else dp))

    def came_over(far, yy, late, n):
        p = piece(1, core, yy, 1 - xl if far else xl, late)
        remote(p, p, ossem.at[far, n], orsem.at[far, n], there(dp)).wait_recv()

    def share(p, yy, other, late, n):
        q, m = piece(p, core, yy, 1 - xl if other else xl, late), 4 * p + 2 * other + late
        send(remote(q, q, cssem.at[m, n], csem.at[m, n], here(cpair)))

    def shared(p, yy, other, late, n):
        q, m = piece(p, 1 - core, yy, 1 - xl if other else xl, late), 4 * p + 2 * other + late
        remote(q, q, cssem.at[m, n], csem.at[m, n], here(cpair)).wait_recv()

    def split(p, cc, yy, xx, late):
        row = pl.multiple_of(((yy * 2 + xx) * 2 + cc) * ROWS, ROWS)
        base = EARLY if late else 0

        def step(m, carry):
            b = 4 * p + (2 if late else 0) + m
            for j in range(T):
                w = jnp.concatenate([G[p, cc, yy, xx, base + m * 2 * T + j], G[p, cc, yy, xx, base + m * 2 * T + T + j]], 0)
                hi = w.astype(BF16)
                lo = (w - hi.astype(F32)).astype(BF16)
                lanes = slice(128 * j, 128 * j + 128)
                W3[b, pl.ds(row, ROWS), lanes] = hi
                W3[b, pl.ds(pl.multiple_of(C + row, ROWS), ROWS), lanes] = hi
                W3[b, pl.ds(pl.multiple_of(2 * C + row, ROWS), ROWS), lanes] = lo
            return carry

        lax.fori_loop(0, 2, step, 0)

    def both(k):
        return (0,) if k in (0, half) else (0, 1)

    def from_core(p, k):
        for way in both(k):
            yy = place(way, k)
            for other in (0, 1):
                for late in (0, 1):
                    shared(p, yy, other, late, slot(way, k))
                    split(p, 1 - core, yy, 1 - xl if other else xl, late)

    def ring_step(streams, k):
        got = []
        for stream in streams:
            for way in (0, 1):
                if not carried(way, stream, k):
                    continue
                yy = arrived(way, stream, k)
                if carried(way, stream, k + 1):
                    send(ring(way, stream, k + 1))
                n = slot(way, k)
                if stream == LATE:
                    send(cross(way, k))
                p = 1 if stream >= TWIN else 0
                share(p, yy, 1 if stream in (PAIR, TWIN_PAIR) else 0, 1 if stream == LATE else 0, n)
                got.append((p, yy, column(stream), stream == LATE))
        for p, yy, xx, late in got:
            split(p, core, yy, xx, late)

    def own_tail(k):
        for way in both(k):
            crossed(way, k)
            share(0, place(way, k), 1, 1, slot(way, k))
            split(0, core, place(way, k), 1 - xl, True)
        from_core(0, k)

    def send_over(k):
        for way in both(k):
            for far in (0, 1):
                send(over(far, place(way, k), True, slot(way, k)))

    def twin_tail(k):
        for way in both(k):
            for far in (0, 1):
                yy = place(way, k)
                came_over(far, yy, True, slot(way, k))
                share(1, yy, far, 1, slot(way, k))
                split(1, core, yy, 1 - xl if far else xl, True)

    own = piece(0, core, y, xl, False)
    send(remote(own, own, xssem.at[Y], xsem.at[Y], here(xpair)))
    for stream in (OWN, LATE):
        for way in (0, 1):
            if carried(way, stream, 1):
                send(ring(way, stream, 1))
    send(cross(0, 0))
    share(0, y, 0, 0, 0)
    share(0, y, 0, 1, 0)
    for far in (0, 1):
        send(over(far, y, False, Y))
    old_copy = remote(pend.at[1], BUF.at[2], mssem.at[2, 0], mrsem.at[2, 0], at(nxt2))

    @pl.when((odd == 1) & (sec < S - 2))
    def _():
        old_copy.start()

    split(0, core, y, xl, False)
    split(0, core, y, xl, True)
    other_own = piece(0, core, y, 1 - xl, False)
    remote(other_own, other_own, xssem.at[Y], xsem.at[Y], here(xpair)).wait_recv()
    for way in (0, 1):
        if carried(way, PAIR, 1):
            send(ring(way, PAIR, 1))
    share(0, y, 1, 0, 0)
    split(0, core, y, 1 - xl, False)

    def start_twin():
        for far in (0, 1):
            came_over(far, y, False, Y)
            for way in (0, 1):
                stream = TWIN_PAIR if far else TWIN
                if carried(way, stream, 1):
                    send(ring(way, stream, 1))
            share(1, y, far, 0, 0)
            split(1, core, y, 1 - xl if far else xl, False)

    LAG = 2
    for k in range(1, half + 1):
        ring_step((LATE, OWN, PAIR), k)
        own_tail(k - 1)
        send_over(k - 1)
        if k == min(LAG, half):
            start_twin()
        if k > LAG:
            ring_step((TWIN, TWIN_PAIR), k - LAG)
    own_tail(half)
    send_over(half)

    lane = lax.broadcasted_iota(jnp.int32, (8, 128), 1) // ROWS

    def gather_taps(p):
        def step(g, carry):
            lanes = pl.ds(pl.multiple_of(g * 128, 128), 128)
            tiles = [G[p, e % 2, 2 * g + e // 4, (e // 2) % 2, EARLY - 1] for e in range(8)]
            for q in range(8):
                row = jnp.zeros((8, 128), F32)
                for e in range(8):
                    shift = ((e - q) % 8) * ROWS
                    moved = pltpu.roll(tiles[e], shift, 1) if shift else tiles[e]
                    row = jnp.where(lane == e, moved, row)
                taps[p, q, :, lanes] = row
            return carry

        lax.fori_loop(0, T, step, 0)

    gather_taps(0)
    for c in local[1:]:
        c.wait()

    @pl.when(sec == 0)
    def _():
        for c in stems_zero:
            c.wait()

    @pl.when(sec == 1)
    def _():
        for c in stems_one:
            c.wait()

    col = lax.broadcasted_iota(jnp.int32, (1, GRID, KC), 1)

    def depthwise(v, p, b, kc, acts):
        def tap(t):
            n = 9 * b + t
            return taps[p, n % 8, n // 8:n // 8 + 1, kc * KC:(kc + 1) * KC].reshape(1, 1, KC)

        v = jnp.maximum(v.reshape(GRID, GRID, KC), 0.0)
        left, right = pltpu.roll(v, 1, 1), pltpu.roll(v, GRID - 1, 1)
        rows = []
        for i in range(3):
            kl = jnp.where(col == 0, 0.0, jnp.broadcast_to(tap(3 * i), (1, GRID, KC)))
            kr = jnp.where(col == GRID - 1, 0.0, jnp.broadcast_to(tap(3 * i + 2), (1, GRID, KC)))
            rows.append(left * kl + v * tap(3 * i + 1) + right * kr)
        zero = jnp.zeros((1, GRID, KC), F32)
        total = (jnp.concatenate([zero, rows[0][:GRID - 1]], 0) + rows[1]
                 + jnp.concatenate([rows[2][1:], zero], 0)).reshape(PIX, KC)
        hi = total.astype(BF16)
        lo = (total - hi.astype(F32)).astype(BF16)
        acts[:, kc * KC:(kc + 1) * KC] = hi
        acts[:, C + kc * KC:C + (kc + 1) * KC] = lo
        acts[:, 2 * C + kc * KC:2 * C + (kc + 1) * KC] = hi

    part = lambda nc: slice(nc * KC, (nc + 1) * KC)
    span = lambda nc: pl.ds(nc * KC, KC)

    def landed(m, nc):
        r = BUF.at[m, :, span(nc)]
        remote(r, r, mssem.at[m, nc], mrsem.at[m, nc], at(prv)).wait_recv()

    def pass_on(t, m, nc, dev):
        return remote(BUF.at[8 + t, :, span(nc)], BUF.at[m, :, span(nc)], mssem.at[m, nc], mrsem.at[m, nc], dev)

    up0 = lambda nc: pass_on(0, 4 - odd, nc, at(nxt2))
    up1 = lambda nc: pass_on(1, 5, nc, at(nxt2))
    up2 = lambda nc: pass_on(2, 7, nc, at(nxt))
    home = remote(BUF.at[9], OUT.at[1], mssem.at[8, 0], mrsem.at[8, 0], there(dp))
    again = remote(OUT.at[1], BUF.at[6], mssem.at[6, 0], mrsem.at[6, 0], at(nxt2))

    def cell(t, p):
        ear = jnp.where(t == 0, 0, jnp.where(t == 1, 1 + odd, jnp.where(t == 2, 4 - odd, 6)))
        new = jnp.where(t == 0, 1, jnp.where(t == 1, 8 - 5 * odd, jnp.where(t == 2, 5 + 4 * odd, 7)))

        def product(acts, b, nc):
            return jnp.dot(acts[...], W3[4 * p + b, :, nc * KC:(nc + 1) * KC], preferred_element_type=F32)

        @pl.when((t == 1) & (odd == 1) & (sec > 1))
        def _():
            r = BUF.at[2]
            remote(r, r, mssem.at[2, 0], mrsem.at[2, 0], at(prv2)).wait_recv()

        @pl.when((t == 2) & (odd == 0) & (sec > 1))
        def _():
            landed(4, 0)
            landed(4, 1)

        @pl.when((t == 3) & (sec > 1))
        def _():
            r = BUF.at[6]
            remote(r, r, mssem.at[6, 0], mrsem.at[6, 0], at(prv2)).wait_recv()

        for kc in (0, 1):
            depthwise(BUF[ear, :, part(kc)], p, 1, kc, B3)
        for nc in (0, 1):
            first[:, part(nc)] = product(B3, 1, nc)
        for kc in (0, 1):
            @pl.when((t == 1) & (odd == 1) & (sec > 1))
            def _():
                landed(3, kc)

            @pl.when((t == 2) & (odd == 0) & (sec > 1))
            def _():
                landed(5, kc)

            @pl.when((t == 3) & (sec > 0))
            def _():
                landed(7, kc)

            depthwise(BUF[new, :, part(kc)], p, 0, kc, A3)
        for nc in (0, 1):
            first[:, part(nc)] += product(A3, 0, nc)
        for kc in (0, 1):
            depthwise(first[:, part(kc)], p, 2, kc, B3)
        for nc in (0, 1):
            second[:, part(nc)] = product(B3, 2, nc) + BUF[new, :, part(nc)]
        for kc in (0, 1):
            depthwise(second[:, part(kc)], p, 3, kc, A3)
        for nc in (0, 1):
            v = product(A3, 3, nc) + first[:, part(nc)]
            BUF[8 + t, :, part(nc)] = v

            @pl.when(t != 1)
            def _():
                OUT[t, :, part(nc)] = v

            @pl.when((t == 0) & (sec < S - 2))
            def _():
                up0(nc).start()

            @pl.when((t == 1) & (odd == 0) & (sec < S - 2))
            def _():
                up1(nc).start()

            @pl.when((t == 2) & (sec < S - 1))
            def _():
                up2(nc).start()

        @pl.when(t == 1)
        def _():
            home.start()

        @pl.when(t == 2)
        def _():
            home.wait_recv()

        @pl.when((t == 2) & (sec < S - 2))
        def _():
            again.start()

    cell(jnp.int32(0), 0)

    for k in range(max(half - LAG, 0) + 1, half + 1):
        ring_step((TWIN, TWIN_PAIR), k)
    for k in range(half + 1):
        twin_tail(k)
    for k in range(half + 1):
        from_core(1, k)
    gather_taps(1)

    def tick(t, carry):
        cell(t, jnp.where(t == 1, 1, 0))
        return carry

    lax.fori_loop(1, TICKS, tick, 0)

    for c in sent:
        c.wait_send()
    home.wait_send()

    @pl.when((odd == 1) & (sec < S - 2))
    def _():
        old_copy.wait_send()

    @pl.when(sec < S - 2)
    def _():
        for nc in (0, 1):
            up0(nc).wait_send()
        again.wait_send()

    @pl.when((odd == 0) & (sec < S - 2))
    def _():
        for nc in (0, 1):
            up1(nc).wait_send()

    @pl.when(sec < S - 1)
    def _():
        for nc in (0, 1):
            up2(nc).wait_send()


def body(S, Y, pend, stem, spatial, mixing):
    C = mixing.shape[-1]
    T = C // 128
    pend = pend.reshape(2, PIX, C)
    stem = stem.reshape(TICKS - 1, PIX, C)
    flat = jnp.pad(spatial.reshape(36, ROWS), ((0, 28), (0, 0))).reshape(1, 8, 128)
    tiles = mixing.reshape(4, 2, 8, T, 128).transpose(0, 1, 3, 2, 4).reshape(8 * T, 8, 128)
    blk = jnp.concatenate([tiles[:4 * T], flat, tiles[4 * T:]], 0)
    dma = pltpu.SemaphoreType.DMA
    any_ = pl.BlockSpec(memory_space=pl.ANY)
    half = Y // 2
    out = pl.pallas_call(
        functools.partial(kernel, S, Y, C),
        out_shape=jax.ShapeDtypeStruct((TICKS, PIX, C), F32),
        in_specs=[any_] * 3,
        out_specs=pl.BlockSpec(memory_space=pltpu.VMEM),
        scratch_shapes=[
            pltpu.VMEM((2, 2, Y, 2, 8 * T + 1, 8, 128), F32),
            pltpu.VMEM((8, 3 * C, C), BF16),
            pltpu.VMEM((PIX, 3 * C), BF16),
            pltpu.VMEM((PIX, 3 * C), BF16),
            pltpu.VMEM((2, 8, 8, C), F32),
            pltpu.VMEM((12, PIX, C), F32),
            pltpu.VMEM((PIX, C), F32),
            pltpu.VMEM((PIX, C), F32),
            dma((13,)),
            dma((2, 5, half)),
            dma((2, 5, half)),
            dma((Y + 1,)),
            dma((Y + 1,)),
            dma((2, Y + 1)),
            dma((2, Y + 1)),
            dma((8, Y)),
            dma((8, Y)),
            dma((9, 2)),
            dma((9, 2)),
        ],
        compiler_params=pltpu.CompilerParams(collective_id=0, has_side_effects=True, vmem_limit_bytes=38 << 20),
        name="relay",
    )(pend, stem, blk)
    return out.reshape(1, TICKS, 1, GRID, GRID, C)


def solution(mesh):
    S, D = mesh.shape["section"], mesh.shape["dp"]
    placed = (
        P("section", None, "dp", None, None, None),
        P(None, "dp", None, None, None),
        P("section", None, None, "dp"),
        P("section", None, "dp", None),
    )
    return jax.shard_map(
        functools.partial(body, S, D // 4),
        mesh=mesh,
        in_specs=placed,
        out_specs=P("section", None, "dp", None, None, None),
        check_vma=False,
    )
```

time: 112 us -> 108 us (0.964)
  the two profiles are of different devices: /device:TPU:384 before, /device:TPU:128 now
where the time goes in v2:
time: 108 us; the launch traced here: 107 us
  Pallas kernels  102 us (94%)
  local copies, waits for them, and re-layouts  5.65 us (5%)
    pallas_call x1, Pallas kernels, body(): pl.pallas_call(functools.partial(kernel, S, Y, C), out_shape=jax.ShapeDty...  102 us
    unnamed x7, local copies, waits for them, and re-layouts  4.68 us

profile of v2, /device:TPU:128, one launch (start us, length us, event | category | flops | bytes accessed | tf_op | source)
XLA Modules:
  0.0 107.5 jit_solution(14478224282950736974)
XLA Ops:
  0.0 0.7 copy.10
  0.7 0.1 reshape.25
  0.8 0.9 fusion
  1.7 0.0 copy-start
  1.7 1.4 %copy-done = f32[3,1,16,16,512]{4,3,2,1,0:T(8,128)S(1)} copy-done((f32[3,1,16,16,512]{4,3,2,1,0:T(8,128)S(1)}, f32[3,1,16,16,512]{4,3,2,1,0:T(8,128)}, u32[]{:S(2)}) %copy-start) | copy-done | bytes 1572888
  3.1 0.0 copy-start.1
  3.1 1.2 %copy-done.1 = f32[1,2,1,16,16,512]{5,4,3,2,1,0:T(8,128)S(1)} copy-done((f32[1,2,1,16,16,512]{5,4,3,2,1,0:T(8,128)S(1)}, f32[1,2,1,16,16,512]{5,4,3,2,1,0:T(8,128)}, u32[]{:S(2)}) %copy-start.1) | copy-done | bytes 1048600
  4.4 101.8 %relay.1 = f32[4,256,512]{2,1,0:T(8,128)S(1)} custom-call(f32[2,256,512]{2,1,0:T(8,128)S(1)} %bitcast.12, f32[3,256,512]{2,1,0:T(8,128)S(1)} %bitcast.11, f32[33,8,128]{2,1,0:T(8,128)S(1)} %pad_maximum_fusion.blk), custom_call_target="tpu_custom_call" | custom-call | tf_op jit(solution)/shard_map/relay/pallas_call | solution.py:446
  106.2 1.3 %copy.13 = f32[1,4,1,16,16,512]{5,4,3,2,1,0:T(8,128)} copy(f32[1,4,1,16,16,512]{5,4,3,2,1,0:T(8,128)S(1)} %bitcast.10) | data formatting | bytes 4194304
  (3 shorter events, 0.0 us)
Async XLA Ops:
  1.7 1.4 %copy-start = (f32[3,1,16,16,512]{4,3,2,1,0:T(8,128)S(1)}, f32[3,1,16,16,512]{4,3,2,1,0:T(8,128)}, u32[]{:S(2)}) copy-start(f32[3,1,16,16,512]{4,3,2,1,0:T(8,128)} %param.5) | copy-start | bytes 4718596
  3.1 1.2 %copy-start.1 = (f32[1,2,1,16,16,512]{5,4,3,2,1,0:T(8,128)S(1)}, f32[1,2,1,16,16,512]{5,4,3,2,1,0:T(8,128)}, u32[]{:S(2)}) copy-start(f32[1,2,1,16,16,512]{5,4,3,2,1,0:T(8,128)} %param.4) | copy-start | bytes 3145732

commit v3 on v2

--- a/solution.py
+++ b/solution.py
@@ -309,7 +309,8 @@
     up1 = lambda nc: pass_on(1, 5, nc, at(nxt2))
     up2 = lambda nc: pass_on(2, 7, nc, at(nxt))
     home = remote(BUF.at[9], OUT.at[1], mssem.at[8, 0], mrsem.at[8, 0], there(dp))
-    again = remote(OUT.at[1], BUF.at[6], mssem.at[6, 0], mrsem.at[6, 0], at(nxt2))
+    again = lambda nc: remote(OUT.at[1, :, span(nc)], BUF.at[6, :, span(nc)], mssem.at[6, nc], mrsem.at[6, nc], at(nxt2))
+    aside = remote(BUF.at[5, :, span(1)], BUF.at[6, :, span(1)], mssem.at[8, 1], mrsem.at[6, 1], there(dp))
 
     def cell(t, p):
         ear = jnp.where(t == 0, 0, jnp.where(t == 1, 1 + odd, jnp.where(t == 2, 4 - odd, 6)))
@@ -330,8 +331,8 @@
 
         @pl.when((t == 3) & (sec > 1))
         def _():
-            r = BUF.at[6]
-            remote(r, r, mssem.at[6, 0], mrsem.at[6, 0], at(prv2)).wait_recv()
+            landed(6, 0)
+            landed(6, 1)
 
         for kc in (0, 1):
             depthwise(BUF[ear, :, part(kc)], p, 1, kc, B3)
@@ -345,6 +346,8 @@
             @pl.when((t == 2) & (odd == 0) & (sec > 1))
             def _():
                 landed(5, kc)
+                if kc == 1:
+                    aside.start()
 
             @pl.when((t == 3) & (sec > 0))
             def _():
@@ -375,6 +378,11 @@
             def _():
                 up1(nc).start()
 
+            if nc == 0:
+                @pl.when(t == 2)
+                def _():
+                    home.wait_send()
+
             @pl.when((t == 2) & (sec < S - 1))
             def _():
                 up2(nc).start()
@@ -389,7 +397,11 @@
 
         @pl.when((t == 2) & (sec < S - 2))
         def _():
-            again.start()
+            again(0).start()
+
+        @pl.when((t == 2) & (odd == 0) & (sec < S - 2))
+        def _():
+            again(1).start()
 
     cell(jnp.int32(0), 0)
 
@@ -409,7 +421,6 @@
 
     for c in sent:
         c.wait_send()
-    home.wait_send()
 
     @pl.when((odd == 1) & (sec < S - 2))
     def _():
@@ -419,10 +430,15 @@
     def _():
         for nc in (0, 1):
             up0(nc).wait_send()
-        again.wait_send()
+        again(0).wait_send()
+
+    @pl.when((odd == 0) & (sec > 1))
+    def _():
+        aside.wait_send()
 
     @pl.when((odd == 0) & (sec < S - 2))
     def _():
+        again(1).wait_send()
         for nc in (0, 1):
             up1(nc).wait_send()
 

time: 108 us -> 110 us (1.019)
  the two profiles are of different devices: /device:TPU:128 before, /device:TPU:132 now
where the time goes in v3:
time: 110 us
  Pallas kernels  104 us (95%)
  local copies, waits for them, and re-layouts  5.65 us (5%)
    pallas_call x1, Pallas kernels, body(): pl.pallas_call(functools.partial(kernel, S, Y, C), out_shape=jax.ShapeDty...  104 us
    unnamed x7, local copies, waits for them, and re-layouts  4.68 us

profile of v3, /device:TPU:132, one launch (start us, length us, event | category | flops | bytes accessed | tf_op | source)
XLA Modules:
  0.0 109.5 jit_solution(7004703712437868907)
XLA Ops:
  0.0 0.7 copy.10
  0.7 0.1 reshape.25
  0.8 0.9 fusion
  1.7 0.0 copy-start
  1.7 1.4 %copy-done = f32[3,1,16,16,512]{4,3,2,1,0:T(8,128)S(1)} copy-done((f32[3,1,16,16,512]{4,3,2,1,0:T(8,128)S(1)}, f32[3,1,16,16,512]{4,3,2,1,0:T(8,128)}, u32[]{:S(2)}) %copy-start) | copy-done | bytes 1572888
  3.1 0.0 copy-start.1
  3.1 1.2 %copy-done.1 = f32[1,2,1,16,16,512]{5,4,3,2,1,0:T(8,128)S(1)} copy-done((f32[1,2,1,16,16,512]{5,4,3,2,1,0:T(8,128)S(1)}, f32[1,2,1,16,16,512]{5,4,3,2,1,0:T(8,128)}, u32[]{:S(2)}) %copy-start.1) | copy-done | bytes 1048600
  4.4 103.8 %relay.1 = f32[4,256,512]{2,1,0:T(8,128)S(1)} custom-call(f32[2,256,512]{2,1,0:T(8,128)S(1)} %bitcast.12, f32[3,256,512]{2,1,0:T(8,128)S(1)} %bitcast.11, f32[33,8,128]{2,1,0:T(8,128)S(1)} %pad_maximum_fusion.blk), custom_call_target="tpu_custom_call" | custom-call | tf_op jit(solution)/shard_map/relay/pallas_call | solution.py:462
  108.2 1.3 %copy.13 = f32[1,4,1,16,16,512]{5,4,3,2,1,0:T(8,128)} copy(f32[1,4,1,16,16,512]{5,4,3,2,1,0:T(8,128)S(1)} %bitcast.10) | data formatting | bytes 4194304
  (3 shorter events, 0.0 us)
Async XLA Ops:
  1.7 1.4 %copy-start = (f32[3,1,16,16,512]{4,3,2,1,0:T(8,128)S(1)}, f32[3,1,16,16,512]{4,3,2,1,0:T(8,128)}, u32[]{:S(2)}) copy-start(f32[3,1,16,16,512]{4,3,2,1,0:T(8,128)} %param.5) | copy-start | bytes 4718596
  3.1 1.2 %copy-start.1 = (f32[1,2,1,16,16,512]{5,4,3,2,1,0:T(8,128)S(1)}, f32[1,2,1,16,16,512]{5,4,3,2,1,0:T(8,128)}, u32[]{:S(2)}) copy-start(f32[1,2,1,16,16,512]{5,4,3,2,1,0:T(8,128)} %param.4) | copy-start | bytes 3145732

commit v4 on v3

--- a/solution.py
+++ b/solution.py
@@ -324,6 +324,10 @@
             r = BUF.at[2]
             remote(r, r, mssem.at[2, 0], mrsem.at[2, 0], at(prv2)).wait_recv()
 
+        @pl.when((t == 2) & (sec < 2))
+        def _():
+            home.wait_recv()
+
         @pl.when((t == 2) & (odd == 0) & (sec > 1))
         def _():
             landed(4, 0)
@@ -391,7 +395,7 @@
         def _():
             home.start()
 
-        @pl.when(t == 2)
+        @pl.when((t == 2) & (sec > 1))
         def _():
             home.wait_recv()
 

time: 110 us -> 103 us (0.936)
  the two profiles are of different devices: /device:TPU:132 before, /device:TPU:70 now
where the time goes in v4:
time: 103 us; the launch traced here: 102 us
  Pallas kernels  96.6 us (94%)
  local copies, waits for them, and re-layouts  5.65 us (5%)
    pallas_call x1, Pallas kernels, body(): pl.pallas_call(functools.partial(kernel, S, Y, C), out_shape=jax.ShapeDty...  96.6 us
    unnamed x7, local copies, waits for them, and re-layouts  4.68 us

profile of v4, /device:TPU:70, one launch (start us, length us, event | category | flops | bytes accessed | tf_op | source)
XLA Modules:
  0.0 102.3 jit_solution(1001072741808599472)
XLA Ops:
  0.0 0.7 copy.10
  0.7 0.1 reshape.25
  0.8 0.9 fusion
  1.7 0.0 copy-start
  1.7 1.4 %copy-done = f32[3,1,16,16,512]{4,3,2,1,0:T(8,128)S(1)} copy-done((f32[3,1,16,16,512]{4,3,2,1,0:T(8,128)S(1)}, f32[3,1,16,16,512]{4,3,2,1,0:T(8,128)}, u32[]{:S(2)}) %copy-start) | copy-done | bytes 1572888
  3.1 0.0 copy-start.1
  3.1 1.2 %copy-done.1 = f32[1,2,1,16,16,512]{5,4,3,2,1,0:T(8,128)S(1)} copy-done((f32[1,2,1,16,16,512]{5,4,3,2,1,0:T(8,128)S(1)}, f32[1,2,1,16,16,512]{5,4,3,2,1,0:T(8,128)}, u32[]{:S(2)}) %copy-start.1) | copy-done | bytes 1048600
  4.4 96.6 %relay.1 = f32[4,256,512]{2,1,0:T(8,128)S(1)} custom-call(f32[2,256,512]{2,1,0:T(8,128)S(1)} %bitcast.12, f32[3,256,512]{2,1,0:T(8,128)S(1)} %bitcast.11, f32[33,8,128]{2,1,0:T(8,128)S(1)} %pad_maximum_fusion.blk), custom_call_target="tpu_custom_call" | custom-call | tf_op jit(solution)/shard_map/relay/pallas_call | solution.py:466
  101.0 1.3 %copy.13 = f32[1,4,1,16,16,512]{5,4,3,2,1,0:T(8,128)} copy(f32[1,4,1,16,16,512]{5,4,3,2,1,0:T(8,128)S(1)} %bitcast.10) | data formatting | bytes 4194304
  (3 shorter events, 0.0 us)
Async XLA Ops:
  1.7 1.4 %copy-start = (f32[3,1,16,16,512]{4,3,2,1,0:T(8,128)S(1)}, f32[3,1,16,16,512]{4,3,2,1,0:T(8,128)}, u32[]{:S(2)}) copy-start(f32[3,1,16,16,512]{4,3,2,1,0:T(8,128)} %param.5) | copy-start | bytes 4718596
  3.1 1.2 %copy-start.1 = (f32[1,2,1,16,16,512]{5,4,3,2,1,0:T(8,128)S(1)}, f32[1,2,1,16,16,512]{5,4,3,2,1,0:T(8,128)}, u32[]{:S(2)}) copy-start(f32[1,2,1,16,16,512]{5,4,3,2,1,0:T(8,128)} %param.4) | copy-start | bytes 3145732

commit v5 on v4

--- a/solution.py
+++ b/solution.py
@@ -240,6 +240,8 @@
             ring_step((TWIN, TWIN_PAIR), k - LAG)
     own_tail(half)
     send_over(half)
+    early = max(half - LAG, 0) + 1
+    ring_step((TWIN, TWIN_PAIR), early)
 
     lane = lax.broadcasted_iota(jnp.int32, (8, 128), 1) // ROWS
 
@@ -409,7 +411,7 @@
 
     cell(jnp.int32(0), 0)
 
-    for k in range(max(half - LAG, 0) + 1, half + 1):
+    for k in range(early + 1, half + 1):
         ring_step((TWIN, TWIN_PAIR), k)
     for k in range(half + 1):
         twin_tail(k)

time: 103 us -> 104 us (level)
  the two profiles are of different devices: /device:TPU:70 before, /device:TPU:152 now
where the time goes in v5:
time: 104 us
  Pallas kernels  98.4 us (95%)
  local copies, waits for them, and re-layouts  5.65 us (5%)
    pallas_call x1, Pallas kernels, body(): pl.pallas_call(functools.partial(kernel, S, Y, C), out_shape=jax.ShapeDty...  98.4 us
    unnamed x7, local copies, waits for them, and re-layouts  4.68 us

profile of v5, /device:TPU:152, one launch (start us, length us, event | category | flops | bytes accessed | tf_op | source)
XLA Modules:
  0.0 104.0 jit_solution(18243240366128874240)
XLA Ops:
  0.0 0.7 copy.10
  0.7 0.1 reshape.25
  0.8 0.9 fusion
  1.7 0.0 copy-start
  1.7 1.4 %copy-done = f32[3,1,16,16,512]{4,3,2,1,0:T(8,128)S(1)} copy-done((f32[3,1,16,16,512]{4,3,2,1,0:T(8,128)S(1)}, f32[3,1,16,16,512]{4,3,2,1,0:T(8,128)}, u32[]{:S(2)}) %copy-start) | copy-done | bytes 1572888
  3.1 0.0 copy-start.1
  3.1 1.2 %copy-done.1 = f32[1,2,1,16,16,512]{5,4,3,2,1,0:T(8,128)S(1)} copy-done((f32[1,2,1,16,16,512]{5,4,3,2,1,0:T(8,128)S(1)}, f32[1,2,1,16,16,512]{5,4,3,2,1,0:T(8,128)}, u32[]{:S(2)}) %copy-start.1) | copy-done | bytes 1048600
  4.4 98.4 %relay.1 = f32[4,256,512]{2,1,0:T(8,128)S(1)} custom-call(f32[2,256,512]{2,1,0:T(8,128)S(1)} %bitcast.12, f32[3,256,512]{2,1,0:T(8,128)S(1)} %bitcast.11, f32[33,8,128]{2,1,0:T(8,128)S(1)} %pad_maximum_fusion.blk), custom_call_target="tpu_custom_call" | custom-call | tf_op jit(solution)/shard_map/relay/pallas_call | solution.py:468
  102.7 1.3 %copy.13 = f32[1,4,1,16,16,512]{5,4,3,2,1,0:T(8,128)} copy(f32[1,4,1,16,16,512]{5,4,3,2,1,0:T(8,128)S(1)} %bitcast.10) | data formatting | bytes 4194304
  (3 shorter events, 0.0 us)
Async XLA Ops:
  1.7 1.4 %copy-start = (f32[3,1,16,16,512]{4,3,2,1,0:T(8,128)S(1)}, f32[3,1,16,16,512]{4,3,2,1,0:T(8,128)}, u32[]{:S(2)}) copy-start(f32[3,1,16,16,512]{4,3,2,1,0:T(8,128)} %param.5) | copy-start | bytes 4718596
  3.1 1.2 %copy-start.1 = (f32[1,2,1,16,16,512]{5,4,3,2,1,0:T(8,128)S(1)}, f32[1,2,1,16,16,512]{5,4,3,2,1,0:T(8,128)}, u32[]{:S(2)}) copy-start(f32[1,2,1,16,16,512]{5,4,3,2,1,0:T(8,128)} %param.4) | copy-start | bytes 3145732

commit v6 on v4

--- a/solution.py
+++ b/solution.py
@@ -409,11 +409,18 @@
 
     cell(jnp.int32(0), 0)
 
-    for k in range(max(half - LAG, 0) + 1, half + 1):
+    done = max(half - LAG, 0)
+    for k in range(done + 1, half):
         ring_step((TWIN, TWIN_PAIR), k)
-    for k in range(half + 1):
+    for k in range(done + 1):
         twin_tail(k)
-    for k in range(half + 1):
+    for k in range(done + 1):
+        from_core(1, k)
+    if done < half:
+        ring_step((TWIN, TWIN_PAIR), half)
+    for k in range(done + 1, half + 1):
+        twin_tail(k)
+    for k in range(done + 1, half + 1):
         from_core(1, k)
     gather_taps(1)
 

time: 103 us -> 102 us (level)
  no operation moved by 1% of the time
where the time goes in v6:
time: 102 us; the launch traced here: 101 us
  Pallas kernels  95.7 us (94%)
  local copies, waits for them, and re-layouts  5.65 us (6%)
    pallas_call x1, Pallas kernels, body(): pl.pallas_call(functools.partial(kernel, S, Y, C), out_shape=jax.ShapeDty...  95.7 us
    unnamed x7, local copies, waits for them, and re-layouts  4.68 us

profile of v6, /device:TPU:70, one launch (start us, length us, event | category | flops | bytes accessed | tf_op | source)
XLA Modules:
  0.0 101.3 jit_solution(4281970511417626799)
XLA Ops:
  0.0 0.7 copy.10
  0.7 0.1 reshape.25
  0.8 0.9 fusion
  1.7 0.0 copy-start
  1.7 1.4 %copy-done = f32[3,1,16,16,512]{4,3,2,1,0:T(8,128)S(1)} copy-done((f32[3,1,16,16,512]{4,3,2,1,0:T(8,128)S(1)}, f32[3,1,16,16,512]{4,3,2,1,0:T(8,128)}, u32[]{:S(2)}) %copy-start) | copy-done | bytes 1572888
  3.1 0.0 copy-start.1
  3.1 1.2 %copy-done.1 = f32[1,2,1,16,16,512]{5,4,3,2,1,0:T(8,128)S(1)} copy-done((f32[1,2,1,16,16,512]{5,4,3,2,1,0:T(8,128)S(1)}, f32[1,2,1,16,16,512]{5,4,3,2,1,0:T(8,128)}, u32[]{:S(2)}) %copy-start.1) | copy-done | bytes 1048600
  4.4 95.7 %relay.1 = f32[4,256,512]{2,1,0:T(8,128)S(1)} custom-call(f32[2,256,512]{2,1,0:T(8,128)S(1)} %bitcast.12, f32[3,256,512]{2,1,0:T(8,128)S(1)} %bitcast.11, f32[33,8,128]{2,1,0:T(8,128)S(1)} %pad_maximum_fusion.blk), custom_call_target="tpu_custom_call" | custom-call | tf_op jit(solution)/shard_map/relay/pallas_call | solution.py:473
  100.0 1.3 %copy.13 = f32[1,4,1,16,16,512]{5,4,3,2,1,0:T(8,128)} copy(f32[1,4,1,16,16,512]{5,4,3,2,1,0:T(8,128)S(1)} %bitcast.10) | data formatting | bytes 4194304
  (3 shorter events, 0.0 us)
Async XLA Ops:
  1.7 1.4 %copy-start = (f32[3,1,16,16,512]{4,3,2,1,0:T(8,128)S(1)}, f32[3,1,16,16,512]{4,3,2,1,0:T(8,128)}, u32[]{:S(2)}) copy-start(f32[3,1,16,16,512]{4,3,2,1,0:T(8,128)} %param.5) | copy-start | bytes 4718596
  3.1 1.2 %copy-start.1 = (f32[1,2,1,16,16,512]{5,4,3,2,1,0:T(8,128)S(1)}, f32[1,2,1,16,16,512]{5,4,3,2,1,0:T(8,128)}, u32[]{:S(2)}) copy-start(f32[1,2,1,16,16,512]{5,4,3,2,1,0:T(8,128)} %param.4) | copy-start | bytes 3145732
